TPU v7x, 32 devices: a whole 2x2x4 slice. The times are simulated.
32 devices in a mesh: blk: 16 (over z, y, core), tok: 2 (over x).
Axes of the slice: x: 2, y: 2, z: 4, core: 2. Of those that a mesh axis runs over, the one named last changes fastest.
Arguments:
- tokens: bfloat16 [64, 8192], P(('blk', 'tok')), may hold values from -6 to 6
- upstream: bfloat16 [64, 8192], P(('blk', 'tok')), may hold values from -6 to 6
- gate_weight: bfloat16 [14336, 8192], P('blk'), may hold values from -0.0625 to 0.0625
- up_weight: bfloat16 [14336, 8192], P('blk'), may hold values from -0.0625 to 0.0625
- down_weight: bfloat16 [14336, 8192], P('blk'), may hold values from -0.046875 to 0.046875
Outputs:
- mixed: bfloat16 [64, 8192], P(('blk', 'tok'))
- input_grad: bfloat16 [64, 8192], P(('blk', 'tok'))
- gate_weight_grad: bfloat16 [14336, 8192], P('blk', 'tok')
- up_weight_grad: bfloat16 [14336, 8192], P('blk', 'tok')
- down_weight_grad: bfloat16 [14336, 8192], P('blk', 'tok')
All inputs are finite; a program needn't handle non-finite values.
Results may differ from a plain program's by a relative error of at most 0.0049.
Values may be sent and summed in bfloat16 or wider, within the bound.
A program may use at most 192 MiB of HBM per device.

v0:
```python
import jax
import jax.numpy as jnp
from jax import lax
from jax.sharding import PartitionSpec as P


def swapped(block, axis, distance):
    count = lax.axis_size(axis)
    route = []
    for low in range(count):
        high = low | 1 << distance
        if high != low and high < count:
            route += [(low, high), (high, low)]
    return lax.ppermute(block, axis, route)


def right_product(left, right):
    return lax.dot_general(
        left, right, (((1,), (1,)), ((), ())), preferred_element_type=jnp.float32
    )


def left_product(left, right):
    return lax.dot_general(
        left, right, (((0,), (0,)), ((), ())), preferred_element_type=jnp.float32
    )


def local(tokens, upstream, gate_weight, up_weight, down_weight):
    rows_in, grads_in = (
        lax.all_gather(tokens, "blk", axis=0, tiled=True),
        lax.all_gather(upstream, "blk", axis=0, tiled=True),
    )
    width = rows_in.shape[1]
    half_width = width // 2
    tok_index = lax.axis_index("tok")
    own_start = tok_index * half_width
    other_start = (1 - tok_index) * half_width
    sent_rows = lax.dynamic_slice_in_dim(rows_in, other_start, half_width, 1)
    sent_grads = lax.dynamic_slice_in_dim(grads_in, other_start, half_width, 1)
    got_rows, got_grads = swapped((sent_rows, sent_grads), "tok", 0)
    gate_value = right_product(rows_in, gate_weight)
    up_value = right_product(rows_in, up_weight)
    gate_sigmoid = jax.nn.sigmoid(gate_value)
    swish_gate = gate_value * gate_sigmoid
    hidden = (swish_gate * up_value).astype(jnp.bfloat16)
    hidden_grad = right_product(grads_in, down_weight)
    gate_grad = (
        hidden_grad * up_value * gate_sigmoid * (1.0 + gate_value * (1.0 - gate_sigmoid))
    ).astype(jnp.bfloat16)
    up_grad = (hidden_grad * swish_gate).astype(jnp.bfloat16)
    output_term = jnp.dot(hidden, down_weight, preferred_element_type=jnp.float32)
    input_term = jnp.dot(gate_grad, gate_weight, preferred_element_type=jnp.float32) + jnp.dot(
        up_grad, up_weight, preferred_element_type=jnp.float32
    )
    summed = lax.psum_scatter(
        jnp.concatenate([output_term, input_term], axis=1), "blk", scatter_dimension=0, tiled=True
    )
    mixed = summed[:, :width].astype(jnp.bfloat16)
    input_grad = summed[:, width:].astype(jnp.bfloat16)
    got_hidden, got_gate, got_up = swapped((hidden, gate_grad, up_grad), "tok", 0)
    own_rows_half = lax.dynamic_slice_in_dim(rows_in, own_start, half_width, 1)
    own_grads_half = lax.dynamic_slice_in_dim(grads_in, own_start, half_width, 1)
    gate_weight_grad = left_product(gate_grad, own_rows_half) + left_product(got_gate, got_rows)
    up_weight_grad = left_product(up_grad, own_rows_half) + left_product(got_up, got_rows)
    down_weight_grad = left_product(hidden, own_grads_half) + left_product(got_hidden, got_grads)
    return (
        mixed,
        input_grad,
        gate_weight_grad.astype(jnp.bfloat16),
        up_weight_grad.astype(jnp.bfloat16),
        down_weight_grad.astype(jnp.bfloat16),
    )


def solution(mesh):
    return jax.shard_map(
        local,
        mesh=mesh,
        in_specs=(
            P(("blk", "tok"), None),
            P(("blk", "tok"), None),
            P("blk", None),
            P("blk", None),
            P("blk", None),
        ),
        out_specs=(
            P(("blk", "tok"), None),
            P(("blk", "tok"), None),
            P("blk", "tok"),
            P("blk", "tok"),
            P("blk", "tok"),
        ),
        check_vma=False,
    )
```

profile of v0, /device:TPU:0, one launch (start us, length us, event | category | flops | bytes accessed | tf_op | source)
XLA Modules:
  0.0 223.9 jit_solution(5780605860671358463)
XLA Ops:
  0.6 24.8 %all-gather = bf16[16,2,8192]{2,1,0:T(2,128)(2,1)S(1)} all-gather(bf16[1,2,8192]{2,1,0:T(2,128)(2,1)} %bitcast.28), channel_id=1, replica_groups=mesh['blk'=16,'tok'=2] {'blk'}, dimensions={0}, use_global_device_ids=true | all-gather | bytes 557056 | tf_op jit(solution)/shard_map/all_gather | solution.py:31
  25.5 0.2 reshape.11
  25.7 0.7 constant_dynamic-slice_fusion.1
  26.4 1.5 collective-permute-start.1
  27.9 9.6 %fusion.11 = f32[32,896]{1,0:T(8,128)S(1)} fusion(bf16[32,8192]{1,0:T(8,128)(2,1)S(1)} %reshape.11, bf16[896,8192]{1,0:T(8,128)(2,1)} %param.7), kind=kOutput, calls=%fused_computation.23 | convolution fusion | flops 469762048 | bytes 15319040 | tf_op jit(solution)/shard_map/dot_general | solution.py:18
  37.5 0.0 copy-done.1
  37.5 18.9 %all-gather.1 = bf16[16,2,8192]{2,1,0:T(2,128)(2,1)S(1)} all-gather(bf16[1,2,8192]{2,1,0:T(2,128)(2,1)S(1)} %bitcast.29), channel_id=1, replica_groups=mesh['blk'=16,'tok'=2] {'blk'}, dimensions={0}, use_global_device_ids=true | all-gather | bytes 557056 | tf_op jit(solution)/shard_map/all_gather | solution.py:32
  56.4 0.2 reshape.13
  56.6 9.6 %fusion.13 = f32[32,896]{1,0:T(8,128)S(1)} fusion(bf16[32,8192]{1,0:T(8,128)(2,1)S(1)} %reshape.13, bf16[896,8192]{1,0:T(8,128)(2,1)} %param.9), kind=kOutput, calls=%fused_computation.25 | convolution fusion | flops 469762048 | bytes 15319040 | tf_op jit(solution)/shard_map/dot_general | solution.py:18
  66.2 9.6 %multiply_convert_fusion.2 = (bf16[32,896]{1,0:T(8,128)(2,1)S(1)}, bf16[32,896]{1,0:T(8,128)(2,1)S(1)}, bf16[32,896]{1,0:T(8,128)(2,1)S(1)}) fusion(f32[32,896]{1,0:T(8,128)S(1)} %fusion.11, f32[32,896]{1,0:T(8,128)S(1)} %fusion.13, bf16[32,8192]{1,0:T(8,128)(2,1)S(1)} %reshape.11, bf16[896,8192]{1,0:T(8,128)(2,1)} %param.8), kind=kOutput, calls=%fused_computation.14 | convolution fusion | flops 470192128 | bytes 15605760 | tf_op jit(solution)/shard_map/dot_general | solution.py:18
  75.8 0.6 collective-permute-start.3
  76.4 1.5 collective-permute-start
  77.9 0.5 collective-permute-start.2
  78.4 0.7 constant_dynamic-slice_fusion
  79.2 1.5 collective-permute-start.4
  80.6 8.8 %fusion.12 = f32[32,8192]{1,0:T(8,128)} fusion(bf16[32,896]{1,0:T(8,128)(2,1)S(1)} %get-tuple-element.5, bf16[896,8192]{1,0:T(8,128)(2,1)} %param.9), kind=kOutput, calls=%fused_computation.24 | convolution fusion | flops 469762048 | bytes 15785984 | tf_op jit(solution)/shard_map/dot_general | solution.py:52
  89.4 7.8 %fusion.14 = f32[32,8192]{1,0:T(8,128)S(1)} fusion(bf16[32,896]{1,0:T(8,128)(2,1)S(1)} %get-tuple-element.6, bf16[896,8192]{1,0:T(8,128)(2,1)} %param.7), kind=kOutput, calls=%fused_computation.26 | convolution fusion | flops 469762048 | bytes 15785984 | tf_op jit(solution)/shard_map/dot_general | solution.py:53
  97.3 0.0 slice-start.1
  97.3 7.6 %fusion = f32[896,4096]{1,0:T(8,128)} fusion(bf16[32,896]{1,0:T(8,128)(2,1)S(1)} %get-tuple-element.5, bf16[32,8192]{1,0:T(8,128)(2,1)S(1)} %reshape.13, s32[]{:T(128)S(6)} %select_n.8), kind=kOutput, calls=%fused_computation.5 | convolution fusion | flops 234881024 | bytes 14999556 | tf_op jit(solution)/shard_map/dot_general | solution.py:24
  104.9 7.3 %fusion.2 = f32[896,4096]{1,0:T(8,128)} fusion(bf16[32,896]{1,0:T(8,128)(2,1)S(1)} %get-tuple-element.7, bf16[32,8192]{1,0:T(8,128)(2,1)S(1)} %reshape.11, s32[]{:T(128)S(6)} %select_n.8), kind=kOutput, calls=%fused_computation.7 | convolution fusion | flops 234881024 | bytes 14999556 | tf_op jit(solution)/shard_map/dot_general | solution.py:24
  112.2 0.0 copy-start.2
  112.2 2.7 %convolution_add_fusion = f32[32,8192]{1,0:T(8,128)S(1)} fusion(f32[32,8192]{1,0:T(8,128)S(1)} %fusion.14, bf16[32,896]{1,0:T(8,128)(2,1)S(1)} %get-tuple-element.7, bf16[896,8192]{1,0:T(8,128)(2,1)S(1)} %bitcast.25), kind=kOutput, calls=%fused_computation.3 | convolution fusion | flops 470024192 | bytes 16834560 | tf_op jit(solution)/shard_map/dot_general | solution.py:53
  114.9 0.0 copy-done
  114.9 0.1 pad_maximum_fusion
  115.1 72.5 %all-reduce.2 = bf16[32,16384]{1,0:T(8,128)(2,1)} all-reduce(f32[32,16384]{1,0:T(8,128)S(1)} %pad_maximum_fusion), channel_id=2, replica_groups=mesh['blk'=16,'tok'=2] {'blk'}, use_global_device_ids=true, to_apply=%region_0.0.clone | all-reduce | flops 524288 | bytes 3145728
  187.6 0.6 dynamic-slice
  188.8 1.0 dynamic-slice_convert_fusion
  189.8 0.7 fusion.10
  190.5 7.2 %fusion.4 = f32[896,4096]{1,0:T(8,128)} fusion(bf16[32,896]{1,0:T(8,128)(2,1)S(1)} %get-tuple-element.6, bf16[32,8192]{1,0:T(8,128)(2,1)S(1)} %reshape.11, s32[]{:T(128)S(6)} %select_n.8), kind=kOutput, calls=%fused_computation.9 | convolution fusion | flops 234881024 | bytes 14999556 | tf_op jit(solution)/shard_map/dot_general | solution.py:24
  197.8 10.5 %add_convert_fusion.1 = bf16[896,4096]{1,0:T(8,128)(2,1)} fusion(f32[896,4096]{1,0:T(8,128)} %fusion.2, bf16[32,896]{1,0:T(8,128)(2,1)S(1)} %collective-permute-done.2, bf16[32,4096]{1,0:T(8,128)(2,1)S(1)} %collective-permute-done.1), kind=kOutput, calls=%fused_computation.1 | convolution fusion | flops 242221056 | bytes 22339584 | tf_op jit(solution)/shard_map/dot_general | solution.py:24
  208.2 10.5 %add_convert_fusion.2 = bf16[896,4096]{1,0:T(8,128)(2,1)} fusion(f32[896,4096]{1,0:T(8,128)} %fusion.4, bf16[32,896]{1,0:T(8,128)(2,1)S(1)} %collective-permute-done, bf16[32,4096]{1,0:T(8,128)(2,1)S(1)} %collective-permute-done.1), kind=kOutput, calls=%fused_computation.2 | convolution fusion | flops 242221056 | bytes 22339584 | tf_op jit(solution)/shard_map/dot_general | solution.py:24
  218.8 5.1 %add_convert_fusion = bf16[896,4096]{1,0:T(8,128)(2,1)} fusion(f32[896,4096]{1,0:T(8,128)S(1)} %bitcast.27, bf16[32,896]{1,0:T(8,128)(2,1)S(1)} %collective-permute-done.3, bf16[32,4096]{1,0:T(8,128)(2,1)S(1)} %collective-permute-done.4), kind=kOutput, calls=%fused_computation | convolution fusion | flops 242221056 | bytes 22339584 | tf_op jit(solution)/shard_map/dot_general | solution.py:24
  (25 shorter events, 0.0 us)
Async XLA Ops:
  0.6 36.9 %copy-start.1 = (bf16[2,8192]{1,0:T(2,128)(2,1)S(1)}, bf16[2,8192]{1,0:T(2,128)(2,1)}, u32[]{:S(2)}) copy-start(bf16[2,8192]{1,0:T(2,128)(2,1)} %param.6) | copy-start | bytes 98308
  26.4 171.4 %collective-permute-start.1 = (bf16[32,4096]{1,0:T(8,128)(2,1)}, bf16[32,4096]{1,0:T(8,128)(2,1)S(1)}, u32[]{:S(2)}, u32[]{:S(2)}) collective-permute-start(bf16[32,4096]{1,0:T(8,128)(2,1)} %constant_dynamic-slice_fusion.1), channel_id=1, source_target_pairs={{0,1},{1,0},{2,3},{3,2},{4,5},{5,4},{6,7},{7,6},{8,9},{9,8},{10,11... | collective-permute-start | bytes 786440 | tf_op jit(solution)/shard_map/ppermute | solution.py:14
  75.8 142.9 %collective-permute-start.3 = (bf16[32,896]{1,0:T(8,128)(2,1)S(1)}, bf16[32,896]{1,0:T(8,128)(2,1)S(1)}, u32[]{:S(2)}, u32[]{:S(2)}) collective-permute-start(bf16[32,896]{1,0:T(8,128)(2,1)S(1)} %get-tuple-element.5), channel_id=1, source_target_pairs={{0,1},{1,0},{2,3},{3,2},{4,5},{5,4},{6,7},{7,6},{8,9},{9,8},{10,11... | collective-permute-start | bytes 172040 | tf_op jit(solution)/shard_map/ppermute | solution.py:14
  76.4 131.8 %collective-permute-start = (bf16[32,896]{1,0:T(8,128)(2,1)S(1)}, bf16[32,896]{1,0:T(8,128)(2,1)S(1)}, u32[]{:S(2)}, u32[]{:S(2)}) collective-permute-start(bf16[32,896]{1,0:T(8,128)(2,1)S(1)} %get-tuple-element.6), channel_id=1, source_target_pairs={{0,1},{1,0},{2,3},{3,2},{4,5},{5,4},{6,7},{7,6},{8,9},{9,8},{10,11... | collective-permute-start | bytes 172040 | tf_op jit(solution)/shard_map/ppermute | solution.py:14
  77.9 119.8 %collective-permute-start.2 = (bf16[32,896]{1,0:T(8,128)(2,1)S(1)}, bf16[32,896]{1,0:T(8,128)(2,1)S(1)}, u32[]{:S(2)}, u32[]{:S(2)}) collective-permute-start(bf16[32,896]{1,0:T(8,128)(2,1)S(1)} %get-tuple-element.7), channel_id=1, source_target_pairs={{0,1},{1,0},{2,3},{3,2},{4,5},{5,4},{6,7},{7,6},{8,9},{9,8},{10,11... | collective-permute-start | bytes 172040 | tf_op jit(solution)/shard_map/ppermute | solution.py:14
  79.2 139.6 %collective-permute-start.4 = (bf16[32,4096]{1,0:T(8,128)(2,1)}, bf16[32,4096]{1,0:T(8,128)(2,1)S(1)}, u32[]{:S(2)}, u32[]{:S(2)}) collective-permute-start(bf16[32,4096]{1,0:T(8,128)(2,1)} %constant_dynamic-slice_fusion), channel_id=1, source_target_pairs={{0,1},{1,0},{2,3},{3,2},{4,5},{5,4},{6,7},{7,6},{8,9},{9,8},{10,11... | collective-permute-start | bytes 786440 | tf_op jit(solution)/shard_map/ppermute | solution.py:14
  97.3 14.9 %slice-start = ((s8[14680064]{0:T(1024)(128)(4,1)}), s8[4194304]{0:T(1024)(128)(4,1)S(1)}, s32[]{:S(2)}) async-start(s8[14680064]{0:T(1024)(128)(4,1)} %bitcast.24), calls=%async_computation | async-start | bytes 8388608
  97.3 14.9 %slice-start.1 = ((s8[14680064]{0:T(1024)(128)(4,1)}), s8[4194304]{0:T(1024)(128)(4,1)S(1)}, s32[]{:S(2)}) async-start(s8[14680064]{0:T(1024)(128)(4,1)} %bitcast.24), calls=%async_computation.1 | async-start | bytes 8388608
  104.9 7.3 %slice-start.2 = ((s8[14680064]{0:T(1024)(128)(4,1)}), s8[4194304]{0:T(1024)(128)(4,1)S(1)}, s32[]{:S(2)}) async-start(s8[14680064]{0:T(1024)(128)(4,1)} %bitcast.24), calls=%async_computation.2 | async-start | bytes 8388608
  104.9 7.3 %slice-start.3 = ((s8[14680064]{0:T(1024)(128)(4,1)}), s8[2097152]{0:T(1024)(128)(4,1)S(1)}, s32[]{:S(2)}) async-start(s8[14680064]{0:T(1024)(128)(4,1)} %bitcast.24), calls=%async_computation.3 | async-start | bytes 4194304
  104.9 10.1 %copy-start = (f32[32,8192]{1,0:T(8,128)S(1)}, f32[32,8192]{1,0:T(8,128)}, u32[]{:S(2)}) copy-start(f32[32,8192]{1,0:T(8,128)} %fusion.12) | copy-start | bytes 3145732
  112.2 75.4 %copy-start.2 = (u32[32]{0:T(128)S(1)}, u32[32]{0:T(128)}, u32[]{:S(2)}) copy-start(u32[32]{0:T(128)} %constant.18) | copy-start | bytes 388
  197.8 21.0 %slice-start.4 = ((s8[14680064]{0:T(1024)(128)(4,1)}), s8[4194304]{0:T(1024)(128)(4,1)S(1)}, s32[]{:S(2)}) async-start(s8[14680064]{0:T(1024)(128)(4,1)} %bitcast.26), calls=%async_computation.4 | async-start | bytes 8388608
  197.8 21.0 %slice-start.5 = ((s8[14680064]{0:T(1024)(128)(4,1)}), s8[4194304]{0:T(1024)(128)(4,1)S(1)}, s32[]{:S(2)}) async-start(s8[14680064]{0:T(1024)(128)(4,1)} %bitcast.26), calls=%async_computation.5 | async-start | bytes 8388608
  208.2 10.5 %slice-start.6 = ((s8[14680064]{0:T(1024)(128)(4,1)}), s8[4194304]{0:T(1024)(128)(4,1)S(1)}, s32[]{:S(2)}) async-start(s8[14680064]{0:T(1024)(128)(4,1)} %bitcast.26), calls=%async_computation.6 | async-start | bytes 8388608
  208.2 10.5 %slice-start.7 = ((s8[14680064]{0:T(1024)(128)(4,1)}), s8[2097152]{0:T(1024)(128)(4,1)S(1)}, s32[]{:S(2)}) async-start(s8[14680064]{0:T(1024)(128)(4,1)} %bitcast.26), calls=%async_computation.7 | async-start | bytes 4194304
where the time goes:
time: 224 us
  blocking collectives  116 us (52%)
  matrix products  96.3 us (43%)
  starting transfers between devices  5.61 us (3%)
  local copies, waits for them, and re-layouts  4.2 us (2%)
    unnamed x1, blocking collectives  72.5 us
    dot_general x6, matrix products, left_product(): lax.dot_general(left, right, (((0,), (0,)), ((), ())), preferred_element_...  48.2 us
    dot_general x3, matrix products, right_product(): lax.dot_general(left, right, (((1,), (1,)), ((), ())), preferred_element_...  28.8 us
    all_gather x1, blocking collectives, local(): lax.all_gather(tokens, 'blk', axis=0, tiled=True)  24.8 us
    all_gather x1, blocking collectives, local(): lax.all_gather(upstream, 'blk', axis=0, tiled=True)  18.9 us
    dot_general x1, matrix products, local(): jnp.dot(hidden, down_weight, preferred_element_type=jnp.float32)  8.78 us
    dot_general x1, matrix products, local(): jnp.dot(gate_grad, gate_weight, preferred_element_type=jnp.float32)  7.84 us
    ppermute x5, starting transfers between devices, swapped(): return lax.ppermute(block, axis, route)  5.61 us
  transfers between devices with their start and end apart: 5, of which 0 were waited for; matrix products, arithmetic and copies ran while one was open for 42% of the time, Pallas kernels for 0%

commit v1 on v0

--- a/solution.py
+++ b/solution.py
@@ -26,19 +26,42 @@
     )
 
 
+def rounds(axis):
+    count = lax.axis_size(axis)
+    levels = count.bit_length() - 1
+    assert count == 1 << levels
+    return range(levels)
+
+
+def gathered(block, axis):
+    for distance in reversed(rounds(axis)):
+        block = jnp.concatenate([block, swapped(block, axis, distance)], axis=0)
+    return block
+
+
+def scattered(term, axis):
+    for distance in rounds(axis):
+        half = term.shape[0] // 2
+        term = term[:half] + swapped(
+            term[half:].astype(jnp.bfloat16), axis, distance
+        ).astype(jnp.float32)
+    return term
+
+
 def local(tokens, upstream, gate_weight, up_weight, down_weight):
-    rows_in, grads_in = (
-        lax.all_gather(tokens, "blk", axis=0, tiled=True),
-        lax.all_gather(upstream, "blk", axis=0, tiled=True),
-    )
+    rows_in = gathered(tokens, "blk")
+    grads_in = gathered(upstream, "blk")
     width = rows_in.shape[1]
     half_width = width // 2
     tok_index = lax.axis_index("tok")
     own_start = tok_index * half_width
     other_start = (1 - tok_index) * half_width
-    sent_rows = lax.dynamic_slice_in_dim(rows_in, other_start, half_width, 1)
-    sent_grads = lax.dynamic_slice_in_dim(grads_in, other_start, half_width, 1)
-    got_rows, got_grads = swapped((sent_rows, sent_grads), "tok", 0)
+
+    def both_groups(rows):
+        own = lax.dynamic_slice_in_dim(rows, own_start, half_width, 1)
+        sent = lax.dynamic_slice_in_dim(rows, other_start, half_width, 1)
+        return jnp.concatenate([own, swapped(sent, "tok", 0)], axis=0)
+
     gate_value = right_product(rows_in, gate_weight)
     up_value = right_product(rows_in, up_weight)
     gate_sigmoid = jax.nn.sigmoid(gate_value)
@@ -53,23 +76,20 @@
     input_term = jnp.dot(gate_grad, gate_weight, preferred_element_type=jnp.float32) + jnp.dot(
         up_grad, up_weight, preferred_element_type=jnp.float32
     )
-    summed = lax.psum_scatter(
-        jnp.concatenate([output_term, input_term], axis=1), "blk", scatter_dimension=0, tiled=True
+    mixed = scattered(output_term, "blk").astype(jnp.bfloat16)
+    input_grad = scattered(input_term, "blk").astype(jnp.bfloat16)
+    all_rows = both_groups(rows_in)
+    all_grads = both_groups(grads_in)
+    all_hidden, all_gate, all_up = (
+        jnp.concatenate([part, swapped(part, "tok", 0)], axis=0)
+        for part in (hidden, gate_grad, up_grad)
     )
-    mixed = summed[:, :width].astype(jnp.bfloat16)
-    input_grad = summed[:, width:].astype(jnp.bfloat16)
-    got_hidden, got_gate, got_up = swapped((hidden, gate_grad, up_grad), "tok", 0)
-    own_rows_half = lax.dynamic_slice_in_dim(rows_in, own_start, half_width, 1)
-    own_grads_half = lax.dynamic_slice_in_dim(grads_in, own_start, half_width, 1)
-    gate_weight_grad = left_product(gate_grad, own_rows_half) + left_product(got_gate, got_rows)
-    up_weight_grad = left_product(up_grad, own_rows_half) + left_product(got_up, got_rows)
-    down_weight_grad = left_product(hidden, own_grads_half) + left_product(got_hidden, got_grads)
     return (
         mixed,
         input_grad,
-        gate_weight_grad.astype(jnp.bfloat16),
-        up_weight_grad.astype(jnp.bfloat16),
-        down_weight_grad.astype(jnp.bfloat16),
+        left_product(all_gate, all_rows).astype(jnp.bfloat16),
+        left_product(all_up, all_rows).astype(jnp.bfloat16),
+        left_product(all_hidden, all_grads).astype(jnp.bfloat16),
     )
 
 

time: 224 us -> 107 us (0.48)
  blocking collectives: 116 us -> 0 us
  matrix products: 96.3 us -> 58.5 us
  starting transfers between devices: 5.61 us -> 25.3 us
  waiting for transfers between devices: 0.01 us -> 13 us
  other arithmetic: 0.14 us -> 6.77 us
  local copies, waits for them, and re-layouts: 4.2 us -> 1.79 us
    unnamed x1 -> x0, blocking collectives: 72.5 us -> none
    all_gather x2 -> x0, blocking collectives: 43.7 us -> none  [the longest x1 24.8 us: local(): lax.all_gather(tokens, 'blk', axis=0, tiled=True)]
    dot_general x6 -> x3, matrix products: 48.2 us -> 15.7 us  [left_product(): lax.dot_general(left, right, (((0,), (0,)), ((), ())), preferred_element_...]
    ppermute x5 -> x21, starting transfers between devices: 5.61 us -> 25.3 us  [swapped(): return lax.ppermute(block, axis, route)]
    ppermute x5 -> x21, waiting for transfers between devices: 0.01 us -> 13 us  [swapped(): return lax.ppermute(block, axis, route)]
    dot_general x1, matrix products: 7.84 us -> 2.69 us  [local(): jnp.dot(gate_grad, gate_weight, preferred_element_type=jnp.float32)]
    concatenate x1 -> x6, other arithmetic: 0.14 us -> 5.26 us  [gathered(): block = jnp.concatenate([block, swapped(block, axis, distance)], axis=0)]
  transfers between devices with their start and end apart: 5 -> 21, of which waited for: 0 -> 9; matrix products, arithmetic and copies ran while one was open for 42% -> 53% of each run, Pallas kernels for 0% -> 0%
where the time goes in v1:
time: 107 us; the launch traced here: 106 us
  matrix products  58.5 us (55%)
  starting transfers between devices  25.3 us (24%)
  waiting for transfers between devices  13 us (12%)
  other arithmetic  6.77 us (6%)
  local copies, waits for them, and re-layouts  1.79 us (2%)
    dot_general x3, matrix products, right_product(): lax.dot_general(left, right, (((1,), (1,)), ((), ())), preferred_element_...  29 us
    ppermute x21, starting transfers between devices, swapped(): return lax.ppermute(block, axis, route)  25.3 us
    dot_general x3, matrix products, left_product(): lax.dot_general(left, right, (((0,), (0,)), ((), ())), preferred_element_...  15.7 us
    ppermute x21, waiting for transfers between devices, swapped(): return lax.ppermute(block, axis, route)  13 us
    dot_general x1, matrix products, local(): jnp.dot(hidden, down_weight, preferred_element_type=jnp.float32)  8.51 us
    concatenate x6, other arithmetic, gathered(): block = jnp.concatenate([block, swapped(block, axis, distance)], axis=0)  5.26 us
    dot_general x1, matrix products, local(): jnp.dot(gate_grad, gate_weight, preferred_element_type=jnp.float32)  2.69 us
    dot_general x1, matrix products, local(): jnp.dot(up_grad, up_weight, preferred_element_type=jnp.float32)  2.69 us
  transfers between devices with their start and end apart: 21, of which 9 were waited for; matrix products, arithmetic and copies ran while one was open for 53% of the time, Pallas kernels for 0%

profile of v1, /device:TPU:0, one launch (start us, length us, event | category | flops | bytes accessed | tf_op | source)
XLA Modules:
  0.0 106.3 jit_solution(434547304285583867)
XLA Ops:
  0.6 4.1 %collective-permute-start = (bf16[2,8192]{1,0:T(2,128)(2,1)}, bf16[2,8192]{1,0:T(2,128)(2,1)S(1)}, u32[]{:S(2)}, u32[]{:S(2)}) collective-permute-start(bf16[2,8192]{1,0:T(2,128)(2,1)} %param.5), channel_id=1, source_target_pairs={{0,16},{16,0},{2,18},{18,2},{4,20},{20,4},{6,22},{22,6},{8,24},{24... | collective-permute-start | bytes 98312 | tf_op jit(solution)/shard_map/ppermute | solution.py:14
  4.8 2.4 %collective-permute-done = bf16[2,8192]{1,0:T(2,128)(2,1)S(1)} collective-permute-done((bf16[2,8192]{1,0:T(2,128)(2,1)}, bf16[2,8192]{1,0:T(2,128)(2,1)S(1)}, u32[]{:S(2)}, u32[]{:S(2)}) %collective-permute-start) | collective-permute-done | bytes 32800 | tf_op jit(solution)/shard_map/ppermute | solution.py:14
  8.1 1.8 %collective-permute-start.1 = (bf16[4,8192]{1,0:T(4,128)(2,1)S(1)}, bf16[4,8192]{1,0:T(4,128)(2,1)S(1)}, u32[]{:S(2)}, u32[]{:S(2)}) collective-permute-start(bf16[4,8192]{1,0:T(4,128)(2,1)S(1)} %pad_maximum_fusion.7), channel_id=1, source_target_pairs={{0,8},{8,0},{2,10},{10,2},{4,12},{12,4},{6,14},{14,6},{16,24},{24,... | collective-permute-start | bytes 196616 | tf_op jit(solution)/shard_map/ppermute | solution.py:14
  10.7 1.6 %collective-permute-start.9 = (bf16[4,8192]{1,0:T(4,128)(2,1)S(1)}, bf16[4,8192]{1,0:T(4,128)(2,1)S(1)}, u32[]{:S(2)}, u32[]{:S(2)}) collective-permute-start(bf16[4,8192]{1,0:T(4,128)(2,1)S(1)} %pad_maximum_fusion.8), channel_id=1, source_target_pairs={{0,8},{8,0},{2,10},{10,2},{4,12},{12,4},{6,14},{14,6},{16,24},{24,... | collective-permute-start | bytes 196616 | tf_op jit(solution)/shard_map/ppermute | solution.py:14
  13.8 2.0 %collective-permute-start.2 = (bf16[8,8192]{1,0:T(8,128)(2,1)S(1)}, bf16[8,8192]{1,0:T(8,128)(2,1)S(1)}, u32[]{:S(2)}, u32[]{:S(2)}) collective-permute-start(bf16[8,8192]{1,0:T(8,128)(2,1)S(1)} %pad_maximum_fusion.5), channel_id=1, source_target_pairs={{0,4},{4,0},{2,6},{6,2},{8,12},{12,8},{10,14},{14,10},{16,20},{20,... | collective-permute-start | bytes 393224 | tf_op jit(solution)/shard_map/ppermute | solution.py:14
  15.7 0.9 pad_maximum_fusion.6
  17.5 2.0 %collective-permute-done.2 = bf16[8,8192]{1,0:T(8,128)(2,1)S(1)} collective-permute-done((bf16[8,8192]{1,0:T(8,128)(2,1)S(1)}, bf16[8,8192]{1,0:T(8,128)(2,1)S(1)}, u32[]{:S(2)}, u32[]{:S(2)}) %collective-permute-start.2) | collective-permute-done | bytes 131104 | tf_op jit(solution)/shard_map/ppermute | solution.py:14
  19.5 0.9 pad_maximum_fusion.3
  20.5 1.1 %collective-permute-done.10 = bf16[8,8192]{1,0:T(8,128)(2,1)S(1)} collective-permute-done((bf16[8,8192]{1,0:T(8,128)(2,1)S(1)}, bf16[8,8192]{1,0:T(8,128)(2,1)S(1)}, u32[]{:S(2)}, u32[]{:S(2)}) %collective-permute-start.10) | collective-permute-done | bytes 131104 | tf_op jit(solution)/shard_map/ppermute | solution.py:14
  21.6 0.9 pad_maximum_fusion.4
  22.7 1.0 concatenate.48
  23.7 9.6 %fusion.19 = f32[32,896]{1,0:T(8,128)S(1)} fusion(bf16[32,8192]{1,0:T(8,128)(2,1)S(1)} %concatenate.48, bf16[896,8192]{1,0:T(8,128)(2,1)} %param.8), kind=kOutput, calls=%fused_computation.54 | convolution fusion | flops 469762048 | bytes 15319040 | tf_op jit(solution)/shard_map/dot_general | solution.py:18
  33.3 9.6 %fusion.18 = f32[32,896]{1,0:T(8,128)S(1)} fusion(bf16[32,8192]{1,0:T(8,128)(2,1)S(1)} %concatenate.48, bf16[896,8192]{1,0:T(8,128)(2,1)} %param.7), kind=kOutput, calls=%fused_computation.53 | convolution fusion | flops 469762048 | bytes 15319040 | tf_op jit(solution)/shard_map/dot_general | solution.py:18
  43.3 9.8 %multiply_convert_fusion = (bf16[32,896]{1,0:T(8,128)(2,1)S(1)}, bf16[32,896]{1,0:T(8,128)(2,1)S(1)}, bf16[32,896]{1,0:T(8,128)(2,1)S(1)}) fusion(f32[32,896]{1,0:T(8,128)S(1)} %fusion.18, f32[32,896]{1,0:T(8,128)S(1)} %fusion.19, bf16[32,8192]{1,0:T(8,128)(2,1)S(1)} %concatenate.52, bf16[896,8192]{1,0:T(8,128)(2,1)} %param.9), kind=kOutput, calls=%fused_computation.33 | convolution fusion | flops 470192128 | bytes 15605760 | tf_op jit(solution)/shard_map/dot_general | solution.py:18
  53.1 1.6 %collective-permute-start.19 = (bf16[32,896]{1,0:T(8,128)(2,1)S(1)}, bf16[32,896]{1,0:T(8,128)(2,1)S(1)}, u32[]{:S(2)}, u32[]{:S(2)}) collective-permute-start(bf16[32,896]{1,0:T(8,128)(2,1)S(1)} %get-tuple-element.11), channel_id=1, source_target_pairs={{0,1},{1,0},{2,3},{3,2},{4,5},{5,4},{6,7},{7,6},{8,9},{9,8},{10,11... | collective-permute-start | bytes 172040 | tf_op jit(solution)/shard_map/ppermute | solution.py:14
  54.7 8.5 %fusion.20 = f32[32,8192]{1,0:T(8,128)S(1)} fusion(bf16[32,896]{1,0:T(8,128)(2,1)S(1)} %get-tuple-element.11, bf16[896,8192]{1,0:T(8,128)(2,1)} %param.9), kind=kOutput, calls=%fused_computation.55 | convolution fusion | flops 469762048 | bytes 15785984 | tf_op jit(solution)/shard_map/dot_general | solution.py:75
  63.4 2.7 %fusion.21 = f32[32,8192]{1,0:T(8,128)S(1)} fusion(bf16[32,896]{1,0:T(8,128)(2,1)S(1)} %get-tuple-element.10, bf16[896,8192]{1,0:T(8,128)(2,1)S(1)} %bitcast.13), kind=kOutput, calls=%fused_computation.56 | convolution fusion | flops 469762048 | bytes 15785984 | tf_op jit(solution)/shard_map/dot_general | solution.py:76
  66.2 2.0 %collective-permute-start.17 = (bf16[32,4096]{1,0:T(8,128)(2,1)S(1)}, bf16[32,4096]{1,0:T(8,128)(2,1)S(1)}, u32[]{:S(2)}, u32[]{:S(2)}) collective-permute-start(bf16[32,4096]{1,0:T(8,128)(2,1)S(1)} %get-tuple-element.8), channel_id=1, source_target_pairs={{0,1},{1,0},{2,3},{3,2},{4,5},{5,4},{6,7},{7,6},{8,9},{9,8},{10,11... | collective-permute-start | bytes 786440 | tf_op jit(solution)/shard_map/ppermute | solution.py:14
  68.4 2.7 %convolution_add_fusion = f32[32,8192]{1,0:T(8,128)S(1)} fusion(f32[32,8192]{1,0:T(8,128)S(1)} %fusion.21, bf16[32,896]{1,0:T(8,128)(2,1)S(1)} %get-tuple-element.9, bf16[896,8192]{1,0:T(8,128)(2,1)S(1)} %bitcast.15), kind=kOutput, calls=%fused_computation | convolution fusion | flops 470024192 | bytes 16834560 | tf_op jit(solution)/shard_map/dot_general | solution.py:76
  71.8 1.1 %collective-permute-done.12 = bf16[16,8192]{1,0:T(8,128)(2,1)S(1)} collective-permute-done((bf16[16,8192]{1,0:T(8,128)(2,1)S(1)}, bf16[16,8192]{1,0:T(8,128)(2,1)S(1)}, u32[]{:S(2)}, u32[]{:S(2)}) %collective-permute-start.12) | collective-permute-done | bytes 262176 | tf_op jit(solution)/shard_map/ppermute | solution.py:14
  72.9 1.9 %collective-permute-start.20 = (bf16[32,4096]{1,0:T(8,128)(2,1)S(1)}, bf16[32,4096]{1,0:T(8,128)(2,1)S(1)}, u32[]{:S(2)}, u32[]{:S(2)}) collective-permute-start(bf16[32,4096]{1,0:T(8,128)(2,1)S(1)} %get-tuple-element.6), channel_id=1, source_target_pairs={{0,1},{1,0},{2,3},{3,2},{4,5},{5,4},{6,7},{7,6},{8,9},{9,8},{10,11... | collective-permute-start | bytes 786440 | tf_op jit(solution)/shard_map/ppermute | solution.py:14
  75.7 1.0 collective-permute-start.5
  76.7 1.0 collective-permute-start.13
  77.7 5.1 %convolution_convert_fusion.1 = bf16[896,4096]{1,0:T(8,128)(2,1)} fusion(bf16[32,4096]{1,0:T(8,128)(2,1)S(1)} %collective-permute-done.17, bf16[32,4096]{1,0:T(8,128)(2,1)S(1)} %get-tuple-element.7, bf16[32,896]{1,0:T(8,128)(2,1)S(1)} %collective-permute-done.18, bf16[32,896]{1,0:T(8,128)(2,1)S(1)} %get-tuple-element.9), kind=kOutput, calls=%fused_computation.2 | convolution fusion | flops 474710016 | bytes 7979008 | tf_op jit(solution)/shard_map/dot_general | solution.py:24
  82.9 5.4 %convolution_convert_fusion.2 = bf16[896,4096]{1,0:T(8,128)(2,1)} fusion(bf16[32,4096]{1,0:T(8,128)(2,1)S(1)} %collective-permute-done.17, bf16[32,4096]{1,0:T(8,128)(2,1)S(1)} %get-tuple-element.7, bf16[32,896]{1,0:T(8,128)(2,1)S(1)} %collective-permute-done.16, bf16[32,896]{1,0:T(8,128)(2,1)S(1)} %get-tuple-element.10), kind=kOutput, calls=%fused_computation.3 | convolution fusion | flops 474710016 | bytes 7979008 | tf_op jit(solution)/shard_map/dot_general | solution.py:24
  88.3 5.2 %convolution_convert_fusion = bf16[896,4096]{1,0:T(8,128)(2,1)} fusion(bf16[32,4096]{1,0:T(8,128)(2,1)S(1)} %collective-permute-done.20, bf16[32,4096]{1,0:T(8,128)(2,1)S(1)} %get-tuple-element.5, bf16[32,896]{1,0:T(8,128)(2,1)S(1)} %collective-permute-done.19, bf16[32,896]{1,0:T(8,128)(2,1)S(1)} %get-tuple-element.11), kind=kOutput, calls=%fused_computation.1 | convolution fusion | flops 474710016 | bytes 7979008 | tf_op jit(solution)/shard_map/dot_general | solution.py:24
  93.5 1.4 %collective-permute-start.6 = (bf16[4,8192]{1,0:T(4,128)(2,1)S(1)}, bf16[4,8192]{1,0:T(4,128)(2,1)S(1)}, u32[]{:S(2)}, u32[]{:S(2)}) collective-permute-start(bf16[4,8192]{1,0:T(4,128)(2,1)S(1)} %slice.113), channel_id=1, source_target_pairs={{0,8},{8,0},{2,10},{10,2},{4,12},{12,4},{6,14},{14,6},{16,24},{24,... | collective-permute-start | bytes 196616 | tf_op jit(solution)/shard_map/ppermute | solution.py:14
  95.7 2.1 %collective-permute-done.6 = bf16[4,8192]{1,0:T(4,128)(2,1)S(1)} collective-permute-done((bf16[4,8192]{1,0:T(4,128)(2,1)S(1)}, bf16[4,8192]{1,0:T(4,128)(2,1)S(1)}, u32[]{:S(2)}, u32[]{:S(2)}) %collective-permute-start.6) | collective-permute-done | bytes 65568 | tf_op jit(solution)/shard_map/ppermute | solution.py:14
  97.9 2.8 %collective-permute-start.7 = (bf16[2,8192]{1,0:T(2,128)(2,1)S(1)}, bf16[2,8192]{1,0:T(2,128)(2,1)S(1)}, u32[]{:S(2)}, u32[]{:S(2)}) collective-permute-start(bf16[2,8192]{1,0:T(2,128)(2,1)S(1)} %slice.115), channel_id=1, source_target_pairs={{0,16},{16,0},{2,18},{18,2},{4,20},{20,4},{6,22},{22,6},{8,24},{24... | collective-permute-start | bytes 98312 | tf_op jit(solution)/shard_map/ppermute | solution.py:14
  100.8 1.5 %collective-permute-start.15 = (bf16[2,8192]{1,0:T(2,128)(2,1)S(1)}, bf16[2,8192]{1,0:T(2,128)(2,1)S(1)}, u32[]{:S(2)}, u32[]{:S(2)}) collective-permute-start(bf16[2,8192]{1,0:T(2,128)(2,1)S(1)} %slice.114), channel_id=1, source_target_pairs={{0,16},{16,0},{2,18},{18,2},{4,20},{20,4},{6,22},{22,6},{8,24},{24... | collective-permute-start | bytes 98312 | tf_op jit(solution)/shard_map/ppermute | solution.py:14
  102.2 0.9 collective-permute-done.7
  103.8 1.8 %collective-permute-done.15 = bf16[2,8192]{1,0:T(2,128)(2,1)S(1)} collective-permute-done((bf16[2,8192]{1,0:T(2,128)(2,1)S(1)}, bf16[2,8192]{1,0:T(2,128)(2,1)S(1)}, u32[]{:S(2)}, u32[]{:S(2)}) %collective-permute-start.15) | collective-permute-done | bytes 32800 | tf_op jit(solution)/shard_map/ppermute | solution.py:14
  (65 shorter events, 9.0 us)
Async XLA Ops:
  0.6 6.6 %collective-permute-start = (bf16[2,8192]{1,0:T(2,128)(2,1)}, bf16[2,8192]{1,0:T(2,128)(2,1)S(1)}, u32[]{:S(2)}, u32[]{:S(2)}) collective-permute-start(bf16[2,8192]{1,0:T(2,128)(2,1)} %param.5), channel_id=1, source_target_pairs={{0,16},{16,0},{2,18},{18,2},{4,20},{20,4},{6,22},{22,6},{8,24},{24... | collective-permute-start | bytes 98312 | tf_op jit(solution)/shard_map/ppermute | solution.py:14
  4.8 5.1 %collective-permute-start.8 = (bf16[2,8192]{1,0:T(2,128)(2,1)}, bf16[2,8192]{1,0:T(2,128)(2,1)S(1)}, u32[]{:S(2)}, u32[]{:S(2)}) collective-permute-start(bf16[2,8192]{1,0:T(2,128)(2,1)} %param.6), channel_id=1, source_target_pairs={{0,16},{16,0},{2,18},{18,2},{4,20},{20,4},{6,22},{22,6},{8,24},{24... | collective-permute-start | bytes 98312 | tf_op jit(solution)/shard_map/ppermute | solution.py:14
  8.1 4.8 %collective-permute-start.1 = (bf16[4,8192]{1,0:T(4,128)(2,1)S(1)}, bf16[4,8192]{1,0:T(4,128)(2,1)S(1)}, u32[]{:S(2)}, u32[]{:S(2)}) collective-permute-start(bf16[4,8192]{1,0:T(4,128)(2,1)S(1)} %pad_maximum_fusion.7), channel_id=1, source_target_pairs={{0,8},{8,0},{2,10},{10,2},{4,12},{12,4},{6,14},{14,6},{16,24},{24,... | collective-permute-start | bytes 196616 | tf_op jit(solution)/shard_map/ppermute | solution.py:14
  10.7 5.1 %collective-permute-start.9 = (bf16[4,8192]{1,0:T(4,128)(2,1)S(1)}, bf16[4,8192]{1,0:T(4,128)(2,1)S(1)}, u32[]{:S(2)}, u32[]{:S(2)}) collective-permute-start(bf16[4,8192]{1,0:T(4,128)(2,1)S(1)} %pad_maximum_fusion.8), channel_id=1, source_target_pairs={{0,8},{8,0},{2,10},{10,2},{4,12},{12,4},{6,14},{14,6},{16,24},{24,... | collective-permute-start | bytes 196616 | tf_op jit(solution)/shard_map/ppermute | solution.py:14
  13.8 5.7 %collective-permute-start.2 = (bf16[8,8192]{1,0:T(8,128)(2,1)S(1)}, bf16[8,8192]{1,0:T(8,128)(2,1)S(1)}, u32[]{:S(2)}, u32[]{:S(2)}) collective-permute-start(bf16[8,8192]{1,0:T(8,128)(2,1)S(1)} %pad_maximum_fusion.5), channel_id=1, source_target_pairs={{0,4},{4,0},{2,6},{6,2},{8,12},{12,8},{10,14},{14,10},{16,20},{20,... | collective-permute-start | bytes 393224 | tf_op jit(solution)/shard_map/ppermute | solution.py:14
  16.6 5.0 %collective-permute-start.10 = (bf16[8,8192]{1,0:T(8,128)(2,1)S(1)}, bf16[8,8192]{1,0:T(8,128)(2,1)S(1)}, u32[]{:S(2)}, u32[]{:S(2)}) collective-permute-start(bf16[8,8192]{1,0:T(8,128)(2,1)S(1)} %pad_maximum_fusion.6), channel_id=1, source_target_pairs={{0,4},{4,0},{2,6},{6,2},{8,12},{12,8},{10,14},{14,10},{16,20},{20,... | collective-permute-start | bytes 393224 | tf_op jit(solution)/shard_map/ppermute | solution.py:14
  20.4 2.2 %collective-permute-start.3 = (bf16[16,8192]{1,0:T(8,128)(2,1)S(1)}, bf16[16,8192]{1,0:T(8,128)(2,1)S(1)}, u32[]{:S(2)}, u32[]{:S(2)}) collective-permute-start(bf16[16,8192]{1,0:T(8,128)(2,1)S(1)} %pad_maximum_fusion.3), channel_id=1, source_target_pairs={{0,2},{2,0},{4,6},{6,4},{8,10},{10,8},{12,14},{14,12},{16,18},{18,... | collective-permute-start | bytes 786440 | tf_op jit(solution)/shard_map/ppermute | solution.py:14
  22.6 20.3 %collective-permute-start.11 = (bf16[16,8192]{1,0:T(8,128)(2,1)S(1)}, bf16[16,8192]{1,0:T(8,128)(2,1)S(1)}, u32[]{:S(2)}, u32[]{:S(2)}) collective-permute-start(bf16[16,8192]{1,0:T(8,128)(2,1)S(1)} %pad_maximum_fusion.4), channel_id=1, source_target_pairs={{0,2},{2,0},{4,6},{6,4},{8,10},{10,8},{12,14},{14,12},{16,18},{18,... | collective-permute-start | bytes 786440 | tf_op jit(solution)/shard_map/ppermute | solution.py:14
  23.7 19.2 %copy-start = (bf16[2,8192]{1,0:T(2,128)(2,1)S(1)}, bf16[2,8192]{1,0:T(2,128)(2,1)}, u32[]{:S(2)}) copy-start(bf16[2,8192]{1,0:T(2,128)(2,1)} %param.6) | copy-start | bytes 98308
  43.3 20.1 %slice-start = ((s8[14680064]{0:T(1024)(128)(4,1)}), s8[4194304]{0:T(1024)(128)(4,1)S(1)}, s32[]{:S(2)}) async-start(s8[14680064]{0:T(1024)(128)(4,1)} %bitcast.12), calls=%async_computation | async-start | bytes 8388608
  43.3 20.1 %slice-start.1 = ((s8[14680064]{0:T(1024)(128)(4,1)}), s8[2097152]{0:T(1024)(128)(4,1)S(1)}, s32[]{:S(2)}) async-start(s8[14680064]{0:T(1024)(128)(4,1)} %bitcast.12), calls=%async_computation.1 | async-start | bytes 4194304
  53.1 10.3 %slice-start.2 = ((s8[14680064]{0:T(1024)(128)(4,1)}), s8[4194304]{0:T(1024)(128)(4,1)S(1)}, s32[]{:S(2)}) async-start(s8[14680064]{0:T(1024)(128)(4,1)} %bitcast.12), calls=%async_computation.2 | async-start | bytes 8388608
  53.1 10.3 %slice-start.3 = ((s8[14680064]{0:T(1024)(128)(4,1)}), s8[4194304]{0:T(1024)(128)(4,1)S(1)}, s32[]{:S(2)}) async-start(s8[14680064]{0:T(1024)(128)(4,1)} %bitcast.12), calls=%async_computation.3 | async-start | bytes 8388608
  53.1 35.1 %collective-permute-start.19 = (bf16[32,896]{1,0:T(8,128)(2,1)S(1)}, bf16[32,896]{1,0:T(8,128)(2,1)S(1)}, u32[]{:S(2)}, u32[]{:S(2)}) collective-permute-start(bf16[32,896]{1,0:T(8,128)(2,1)S(1)} %get-tuple-element.11), channel_id=1, source_target_pairs={{0,1},{1,0},{2,3},{3,2},{4,5},{5,4},{6,7},{7,6},{8,9},{9,8},{10,11... | collective-permute-start | bytes 172040 | tf_op jit(solution)/shard_map/ppermute | solution.py:14
  54.7 13.7 %slice-start.4 = ((s8[14680064]{0:T(1024)(128)(4,1)}), s8[4194304]{0:T(1024)(128)(4,1)S(1)}, s32[]{:S(2)}) async-start(s8[14680064]{0:T(1024)(128)(4,1)} %bitcast.14), calls=%async_computation.4 | async-start | bytes 8388608
  54.7 13.7 %slice-start.5 = ((s8[14680064]{0:T(1024)(128)(4,1)}), s8[4194304]{0:T(1024)(128)(4,1)S(1)}, s32[]{:S(2)}) async-start(s8[14680064]{0:T(1024)(128)(4,1)} %bitcast.14), calls=%async_computation.5 | async-start | bytes 8388608
  63.2 5.2 %slice-start.6 = ((s8[14680064]{0:T(1024)(128)(4,1)}), s8[4194304]{0:T(1024)(128)(4,1)S(1)}, s32[]{:S(2)}) async-start(s8[14680064]{0:T(1024)(128)(4,1)} %bitcast.14), calls=%async_computation.6 | async-start | bytes 8388608
  63.2 5.2 %slice-start.7 = ((s8[14680064]{0:T(1024)(128)(4,1)}), s8[2097152]{0:T(1024)(128)(4,1)S(1)}, s32[]{:S(2)}) async-start(s8[14680064]{0:T(1024)(128)(4,1)} %bitcast.14), calls=%async_computation.7 | async-start | bytes 4194304
  63.2 19.7 %collective-permute-start.16 = (bf16[32,896]{1,0:T(8,128)(2,1)S(1)}, bf16[32,896]{1,0:T(8,128)(2,1)S(1)}, u32[]{:S(2)}, u32[]{:S(2)}) collective-permute-start(bf16[32,896]{1,0:T(8,128)(2,1)S(1)} %get-tuple-element.10), channel_id=1, source_target_pairs={{0,1},{1,0},{2,3},{3,2},{4,5},{5,4},{6,7},{7,6},{8,9},{9,8},{10,11... | collective-permute-start | bytes 172040 | tf_op jit(solution)/shard_map/ppermute | solution.py:14
  66.2 10.5 %collective-permute-start.17 = (bf16[32,4096]{1,0:T(8,128)(2,1)S(1)}, bf16[32,4096]{1,0:T(8,128)(2,1)S(1)}, u32[]{:S(2)}, u32[]{:S(2)}) collective-permute-start(bf16[32,4096]{1,0:T(8,128)(2,1)S(1)} %get-tuple-element.8), channel_id=1, source_target_pairs={{0,1},{1,0},{2,3},{3,2},{4,5},{5,4},{6,7},{7,6},{8,9},{9,8},{10,11... | collective-permute-start | bytes 786440 | tf_op jit(solution)/shard_map/ppermute | solution.py:14
  68.2 7.5 %collective-permute-start.18 = (bf16[32,896]{1,0:T(8,128)(2,1)S(1)}, bf16[32,896]{1,0:T(8,128)(2,1)S(1)}, u32[]{:S(2)}, u32[]{:S(2)}) collective-permute-start(bf16[32,896]{1,0:T(8,128)(2,1)S(1)} %get-tuple-element.9), channel_id=1, source_target_pairs={{0,1},{1,0},{2,3},{3,2},{4,5},{5,4},{6,7},{7,6},{8,9},{9,8},{10,11... | collective-permute-start | bytes 172040 | tf_op jit(solution)/shard_map/ppermute | solution.py:14
  68.3 2.9 %collective-permute-start.4 = (bf16[16,8192]{1,0:T(8,128)(2,1)S(1)}, bf16[16,8192]{1,0:T(8,128)(2,1)S(1)}, u32[]{:S(2)}, u32[]{:S(2)}) collective-permute-start(bf16[16,8192]{1,0:T(8,128)(2,1)S(1)} %slice.109), channel_id=1, source_target_pairs={{0,2},{2,0},{4,6},{6,4},{8,10},{10,8},{12,14},{14,12},{16,18},{18,... | collective-permute-start | bytes 786440 | tf_op jit(solution)/shard_map/ppermute | solution.py:14
  71.2 1.7 %collective-permute-start.12 = (bf16[16,8192]{1,0:T(8,128)(2,1)S(1)}, bf16[16,8192]{1,0:T(8,128)(2,1)S(1)}, u32[]{:S(2)}, u32[]{:S(2)}) collective-permute-start(bf16[16,8192]{1,0:T(8,128)(2,1)S(1)} %slice.108), channel_id=1, source_target_pairs={{0,2},{2,0},{4,6},{6,4},{8,10},{10,8},{12,14},{14,12},{16,18},{18,... | collective-permute-start | bytes 786440 | tf_op jit(solution)/shard_map/ppermute | solution.py:14
  72.9 15.3 %collective-permute-start.20 = (bf16[32,4096]{1,0:T(8,128)(2,1)S(1)}, bf16[32,4096]{1,0:T(8,128)(2,1)S(1)}, u32[]{:S(2)}, u32[]{:S(2)}) collective-permute-start(bf16[32,4096]{1,0:T(8,128)(2,1)S(1)} %get-tuple-element.6), channel_id=1, source_target_pairs={{0,1},{1,0},{2,3},{3,2},{4,5},{5,4},{6,7},{7,6},{8,9},{9,8},{10,11... | collective-permute-start | bytes 786440 | tf_op jit(solution)/shard_map/ppermute | solution.py:14
  75.7 17.7 %collective-permute-start.5 = (bf16[8,8192]{1,0:T(8,128)(2,1)S(1)}, bf16[8,8192]{1,0:T(8,128)(2,1)S(1)}, u32[]{:S(2)}, u32[]{:S(2)}) collective-permute-start(bf16[8,8192]{1,0:T(8,128)(2,1)S(1)} %slice.111), channel_id=1, source_target_pairs={{0,4},{4,0},{2,6},{6,2},{8,12},{12,8},{10,14},{14,10},{16,20},{20,... | collective-permute-start | bytes 393224 | tf_op jit(solution)/shard_map/ppermute | solution.py:14
  76.7 18.2 %collective-permute-start.13 = (bf16[8,8192]{1,0:T(8,128)(2,1)S(1)}, bf16[8,8192]{1,0:T(8,128)(2,1)S(1)}, u32[]{:S(2)}, u32[]{:S(2)}) collective-permute-start(bf16[8,8192]{1,0:T(8,128)(2,1)S(1)} %slice.110), channel_id=1, source_target_pairs={{0,4},{4,0},{2,6},{6,2},{8,12},{12,8},{10,14},{14,10},{16,20},{20,... | collective-permute-start | bytes 393224 | tf_op jit(solution)/shard_map/ppermute | solution.py:14
  93.5 4.3 %collective-permute-start.6 = (bf16[4,8192]{1,0:T(4,128)(2,1)S(1)}, bf16[4,8192]{1,0:T(4,128)(2,1)S(1)}, u32[]{:S(2)}, u32[]{:S(2)}) collective-permute-start(bf16[4,8192]{1,0:T(4,128)(2,1)S(1)} %slice.113), channel_id=1, source_target_pairs={{0,8},{8,0},{2,10},{10,2},{4,12},{12,4},{6,14},{14,6},{16,24},{24,... | collective-permute-start | bytes 196616 | tf_op jit(solution)/shard_map/ppermute | solution.py:14
  95.0 5.7 %collective-permute-start.14 = (bf16[4,8192]{1,0:T(4,128)(2,1)S(1)}, bf16[4,8192]{1,0:T(4,128)(2,1)S(1)}, u32[]{:S(2)}, u32[]{:S(2)}) collective-permute-start(bf16[4,8192]{1,0:T(4,128)(2,1)S(1)} %slice.112), channel_id=1, source_target_pairs={{0,8},{8,0},{2,10},{10,2},{4,12},{12,4},{6,14},{14,6},{16,24},{24,... | collective-permute-start | bytes 196616 | tf_op jit(solution)/shard_map/ppermute | solution.py:14
  97.9 5.2 %collective-permute-start.7 = (bf16[2,8192]{1,0:T(2,128)(2,1)S(1)}, bf16[2,8192]{1,0:T(2,128)(2,1)S(1)}, u32[]{:S(2)}, u32[]{:S(2)}) collective-permute-start(bf16[2,8192]{1,0:T(2,128)(2,1)S(1)} %slice.115), channel_id=1, source_target_pairs={{0,16},{16,0},{2,18},{18,2},{4,20},{20,4},{6,22},{22,6},{8,24},{24... | collective-permute-start | bytes 98312 | tf_op jit(solution)/shard_map/ppermute | solution.py:14
  100.8 4.9 %collective-permute-start.15 = (bf16[2,8192]{1,0:T(2,128)(2,1)S(1)}, bf16[2,8192]{1,0:T(2,128)(2,1)S(1)}, u32[]{:S(2)}, u32[]{:S(2)}) collective-permute-start(bf16[2,8192]{1,0:T(2,128)(2,1)S(1)} %slice.114), channel_id=1, source_target_pairs={{0,16},{16,0},{2,18},{18,2},{4,20},{20,4},{6,22},{22,6},{8,24},{24... | collective-permute-start | bytes 98312 | tf_op jit(solution)/shard_map/ppermute | solution.py:14
